TPU v7x, 32 devices: a whole 2x2x4 slice. The times are simulated.
32 devices in a mesh: dp: 4 (over y, core), tensor: 8 (over z, x).
Axes of the slice: x: 2, y: 2, z: 4, core: 2. Of those that a mesh axis runs over, the one named last changes fastest.
Arguments:
- tokens: bfloat16 [3072, 8192], P('dp', 'tensor'), may hold values from -6 to 6
- cotangent: bfloat16 [3072, 512], P('dp', 'tensor'), may hold values from -0.0625 to 0.0625
- frozen_value_weight: bfloat16 [8192, 512], P('tensor'), may hold values from -0.0625 to 0.0625
- adapter_down_weight: bfloat16 [8, 32, 8192], P('tensor'), may hold values from -0.0625 to 0.0625
- adapter_up_weight: bfloat16 [8, 32, 512], P('tensor'), may hold values from -1 to 1
- member: int32 [24, 1], P('dp'), may hold values from 0 to 7; in each aligned block of 6 rows (0 to 5, 6 to 11, ...) at most 2 rows name the same one
Outputs:
- output: bfloat16 [3072, 512], P(('dp', 'tensor'))
- grad_down: float32 [8, 32, 8192], P('tensor', None, 'dp')
- grad_up: float32 [8, 32, 512], P('tensor', 'dp')
Inputs may be any that keep to these rules, and one draw needn't show every extreme that they name: Within the 6 blocks of one data index no member appears more than 2 times, and some member appears exactly 2 times there.
All inputs are finite; a program needn't handle non-finite values.
Results may differ from a plain program's by a relative error of at most 0.015.
Values may be sent and summed in bfloat16 or wider, within the bound.
A program may use at most 64 MiB of HBM per device.

v0:
```python
import jax
import jax.numpy as jnp
from jax import lax
from jax.sharding import PartitionSpec as P

BLK = 128
CAP = 2
adapter_scale = 2.0
contract_trailing = (((1,), (1,)), ((), ()))
contract_leading = (((0,), (0,)), ((), ()))


def slot_table(member_ids, tensor_size):
    block_total = member_ids.shape[0]
    position = jnp.arange(block_total, dtype=jnp.int32)
    same_member = member_ids[:, None] == member_ids[None, :]
    earlier = position[None, :] < position[:, None]
    slot_rank = jnp.sum(jnp.logical_and(same_member, earlier), axis=1)
    owners = jnp.arange(tensor_size, dtype=jnp.int32)
    slot_numbers = jnp.arange(CAP, dtype=jnp.int32)
    picked = jnp.logical_and(
        member_ids[None, None, :] == owners[:, None, None],
        slot_rank[None, None, :] == slot_numbers[None, :, None],
    )
    return picked.astype(jnp.bfloat16)


def shards(tokens, cotangent, frozen_value_weight, adapter_down_weight, adapter_up_weight, member):
    tensor_size = lax.axis_size("tensor")
    owner_index = lax.axis_index("tensor")
    row_total = tokens.shape[0]
    feature_width = tokens.shape[1]
    cot_width = cotangent.shape[1]
    out_width = frozen_value_weight.shape[1]
    block_total = row_total // BLK
    own_rows = row_total // tensor_size
    member_ids = member[:, 0]
    picked = slot_table(member_ids, tensor_size)
    flat_picked = picked.reshape(tensor_size * CAP, block_total)
    token_blocks = tokens.reshape(block_total, BLK * feature_width)
    cot_blocks = cotangent.reshape(block_total, BLK * cot_width)
    send_tokens = jnp.dot(flat_picked, token_blocks, preferred_element_type=jnp.float32).astype(
        jnp.bfloat16
    )
    send_tokens = send_tokens.reshape(tensor_size, CAP * BLK, feature_width)
    send_cot = jnp.dot(flat_picked, cot_blocks, preferred_element_type=jnp.float32).astype(
        jnp.bfloat16
    )
    send_cot = send_cot.reshape(tensor_size, CAP * BLK, cot_width)
    got_tokens, got_cot = (
        lax.all_to_all(send_tokens, "tensor", split_axis=0, concat_axis=2, tiled=True),
        lax.all_to_all(send_cot, "tensor", split_axis=0, concat_axis=2, tiled=True),
    )
    slot_tokens = got_tokens[0]
    slot_cot = got_cot[0]
    down_projection = adapter_down_weight[0]
    up_projection = adapter_up_weight[0]
    hidden_state = lax.dot_general(
        slot_tokens, down_projection, contract_trailing, preferred_element_type=jnp.float32
    ).astype(jnp.bfloat16)
    adapter_result = (
        adapter_scale * jnp.dot(hidden_state, up_projection, preferred_element_type=jnp.float32)
    ).astype(jnp.bfloat16)
    backward_projection = (
        adapter_scale
        * lax.dot_general(
            slot_cot, up_projection, contract_trailing, preferred_element_type=jnp.float32
        )
    ).astype(jnp.bfloat16)
    local_down = lax.dot_general(
        backward_projection, slot_tokens, contract_leading, preferred_element_type=jnp.float32
    )
    member_up_weight = adapter_scale * lax.dot_general(
        hidden_state, slot_cot, contract_leading, preferred_element_type=jnp.float32
    )
    base_total = lax.psum_scatter(
        jnp.dot(tokens, frozen_value_weight, preferred_element_type=jnp.float32).astype(
            jnp.bfloat16
        ),
        "tensor",
        scatter_dimension=0,
        tiled=True,
    ).astype(jnp.float32)
    my_slots = lax.dynamic_index_in_dim(picked, owner_index, 0, keepdims=False)
    placed = jnp.dot(
        my_slots.T, adapter_result.reshape(CAP, BLK * out_width), preferred_element_type=jnp.float32
    ).astype(jnp.bfloat16)
    placed = placed.reshape(tensor_size, own_rows, out_width)
    returned = lax.all_to_all(placed, "tensor", split_axis=0, concat_axis=0, tiled=True)
    adapter_rows = jnp.sum(returned.astype(jnp.float32), axis=0)
    output = (base_total + adapter_rows).astype(jnp.bfloat16)
    grad_down, grad_up = (
        lax.psum_scatter(
            local_down[None].astype(jnp.bfloat16), "dp", scatter_dimension=2, tiled=True
        ).astype(jnp.float32),
        lax.psum_scatter(
            member_up_weight[None].astype(jnp.bfloat16), "dp", scatter_dimension=1, tiled=True
        ).astype(jnp.float32),
    )
    return (output, grad_down, grad_up)


def solution(mesh):
    placed = (
        P("dp", "tensor"),
        P("dp", "tensor"),
        P("tensor", None),
        P("tensor", None, None),
        P("tensor", None, None),
        P("dp", None),
    )
    return jax.shard_map(
        shards,
        mesh=mesh,
        in_specs=placed,
        out_specs=(P(("dp", "tensor"), None), P("tensor", None, "dp"), P("tensor", "dp", None)),
        check_vma=False,
    )
```

profile of v0, /device:TPU:0, one launch (start us, length us, event | category | flops | bytes accessed | tf_op | source)
XLA Modules:
  0.0 258.6 jit_solution(10288526673390440713)
XLA Ops:
  7.2 0.8 iota_compare_fusion.1
  7.9 0.9 convert_reduce_fusion.1
  8.9 3.4 %reshape.95 = bf16[6,131072]{1,0:T(8,128)(2,1)S(1)} reshape(bf16[768,1024]{1,0:T(8,128)(2,1)} %param.6) | data formatting | bytes 3145728 | tf_op jit(solution)/shard_map/reshape | solution.py:40
  12.2 3.2 %convolution_convert_fusion = bf16[16,131072]{1,0:T(8,128)(2,1)} fusion(pred[16,6]{1,0:T(8,128)(4,1)S(1)} %and.35, bf16[6,131072]{1,0:T(8,128)(2,1)S(1)} %reshape.95), kind=kOutput, calls=%fused_computation | convolution fusion | flops 27262976 | bytes 5767264 | tf_op jit(solution)/shard_map/dot_general | solution.py:42
  15.5 4.8 %reshape.96 = bf16[8,256,1024]{2,1,0:T(8,128)(2,1)} reshape(bf16[16,131072]{1,0:T(8,128)(2,1)} %convolution_convert_fusion) | data formatting | bytes 8388608 | tf_op jit(solution)/shard_map/reshape | solution.py:45
  20.3 6.5 %copy.15 = bf16[8,256,1024]{1,2,0:T(8,128)(2,1)} copy(bf16[8,256,1024]{2,1,0:T(8,128)(2,1)} %reshape.96) | data formatting | bytes 8388608 | tf_op jit(solution)/shard_map/reshape | solution.py:45
  26.8 7.4 %all-to-all-start = ((bf16[8,256,1024]{1,2,0:T(8,128)(2,1)}), bf16[8,256,1024]{1,2,0:T(8,128)(2,1)}, u32[]{:S(2)}, u32[]{:S(2)}) async-start(bf16[8,256,1024]{1,2,0:T(8,128)(2,1)} %copy.15), calls=%async_computation.1 | async-start | bytes 8388608 | tf_op jit(solution)/shard_map/all_to_all | solution.py:51
  34.8 0.5 reshape.100
  35.3 0.9 copy.17
  36.2 91.2 %all-to-all-done = bf16[8,256,1024]{1,2,0:T(8,128)(2,1)} async-done(((bf16[8,256,1024]{1,2,0:T(8,128)(2,1)}), bf16[8,256,1024]{1,2,0:T(8,128)(2,1)}, u32[]{:S(2)}, u32[]{:S(2)}) %all-to-all-start) | async-done | bytes 4194336 | tf_op jit(solution)/shard_map/all_to_all | solution.py:51
  127.5 3.6 %all-to-all-start.2 = ((bf16[8,256,64]{1,2,0:T(8,128)(2,1)}), bf16[8,256,64]{1,2,0:T(8,128)(2,1)S(1)}, u32[]{:S(2)}, u32[]{:S(2)}) async-start(bf16[8,256,64]{1,2,0:T(8,128)(2,1)} %copy.17), calls=%async_computation.3 | async-start | bytes 524288 | tf_op jit(solution)/shard_map/all_to_all | solution.py:52
  131.2 3.1 %convolution_convert_fusion.5 = bf16[256,32]{0,1:T(8,128)(2,1)S(1)} fusion(bf16[256,8192]{0,1:T(8,128)(2,1)} %bitcast.4, bf16[1,32,8192]{2,1,0:T(8,128)(2,1)S(1)} %copy-done.2), kind=kOutput, calls=%fused_computation.14 | convolution fusion | flops 134225920 | bytes 4734976 | tf_op jit(solution)/shard_map/dot_general | solution.py:58
  134.3 5.9 %all-to-all-done.2 = bf16[8,256,64]{1,2,0:T(8,128)(2,1)S(1)} async-done(((bf16[8,256,64]{1,2,0:T(8,128)(2,1)}), bf16[8,256,64]{1,2,0:T(8,128)(2,1)S(1)}, u32[]{:S(2)}, u32[]{:S(2)}) %all-to-all-start.2) | async-done | bytes 262176 | tf_op jit(solution)/shard_map/all_to_all | solution.py:52
  140.2 0.8 fusion.3
  141.1 4.4 %fusion = bf16[1,32,8192]{2,1,0:T(8,128)(2,1)} fusion(bf16[256,8192]{0,1:T(8,128)(2,1)} %bitcast.4, bf16[256,512]{0,1:T(8,128)(2,1)S(1)} %bitcast.41, bf16[1,32,512]{2,1,0:T(8,128)(2,1)S(1)} %copy-done.3), kind=kOutput, calls=%fused_computation.3 | convolution fusion | flops 142884864 | bytes 5013504 | tf_op jit(solution)/shard_map/dot_general | solution.py:70
  145.6 1.9 convolution_convert_fusion.4
  148.5 2.1 reshape.98
  150.5 3.6 %all-to-all-start.1 = ((bf16[8,96,512]{2,1,0:T(8,128)(2,1)}), bf16[8,96,512]{2,1,0:T(8,128)(2,1)S(1)}, u32[]{:S(2)}, u32[]{:S(2)}) async-start(bf16[8,96,512]{2,1,0:T(8,128)(2,1)} %reshape.98), calls=%async_computation.2 | async-start | bytes 1572864 | tf_op jit(solution)/shard_map/all_to_all | solution.py:89
  154.1 5.7 %reduce-scatter.8.cloned.1.call-done = bf16[1,8,512]{2,1,0:T(8,128)(2,1)} async-done(((bf16[1,32,512]{2,1,0:T(8,128)(2,1)}), bf16[1,8,512]{2,1,0:T(8,128)(2,1)}) %reduce-scatter.8.cloned.1.call-update) | async-done | bytes 8208 | tf_op jit(solution)/shard_map/reduce_scatter | solution.py:96
  159.8 1.3 convert_element_type.68
  161.1 22.9 %reduce-scatter.6.cloned.1.call-done = bf16[1,32,2048]{2,1,0:T(8,128)(2,1)} async-done(((bf16[1,32,8192]{2,1,0:T(8,128)(2,1)}), bf16[1,32,2048]{2,1,0:T(8,128)(2,1)}) %reduce-scatter.6.cloned.1.call-update) | async-done | bytes 131088 | tf_op jit(solution)/shard_map/reduce_scatter | solution.py:93
  184.0 1.6 convert_element_type.65
  185.7 64.8 %reduce-scatter.4.cloned.1.call-done = bf16[96,512]{1,0:T(8,128)(2,1)} async-done(((bf16[768,512]{1,0:T(8,128)(2,1)}), bf16[96,512]{1,0:T(8,128)(2,1)}) %reduce-scatter.4.cloned.1.call-update) | async-done | bytes 98320 | tf_op jit(solution)/shard_map/reduce_scatter | solution.py:76
  250.5 1.6 add_convert_fusion
  (27 shorter events, 1.9 us)
Async XLA Ops:
  7.2 138.4 %copy-start = (bf16[1024,512]{1,0:T(8,128)(2,1)S(1)}, bf16[1024,512]{1,0:T(8,128)(2,1)}, u32[]{:S(2)}) copy-start(bf16[1024,512]{1,0:T(8,128)(2,1)} %param.8) | copy-start | bytes 3145732
  26.8 7.4 %copy-start.4 = (bf16[768,64]{0,1:T(8,128)(2,1)S(1)}, bf16[768,64]{0,1:T(8,128)(2,1)}, u32[]{:S(2)}) copy-start(bf16[768,64]{0,1:T(8,128)(2,1)} %param.7) | copy-start | bytes 294916
  26.8 104.4 %copy-start.2 = (bf16[1,32,8192]{2,1,0:T(8,128)(2,1)S(1)}, bf16[1,32,8192]{2,1,0:T(8,128)(2,1)}, u32[]{:S(2)}) copy-start(bf16[1,32,8192]{2,1,0:T(8,128)(2,1)} %param.9) | copy-start | bytes 1572868
  26.8 100.7 %all-to-all-start = ((bf16[8,256,1024]{1,2,0:T(8,128)(2,1)}), bf16[8,256,1024]{1,2,0:T(8,128)(2,1)}, u32[]{:S(2)}, u32[]{:S(2)}) async-start(bf16[8,256,1024]{1,2,0:T(8,128)(2,1)} %copy.15), calls=%async_computation.1 | async-start | bytes 8388608 | tf_op jit(solution)/shard_map/all_to_all | solution.py:51
  34.2 106.9 %copy-start.3 = (bf16[1,32,512]{2,1,0:T(8,128)(2,1)S(1)}, bf16[1,32,512]{2,1,0:T(8,128)(2,1)}, u32[]{:S(2)}) copy-start(bf16[1,32,512]{2,1,0:T(8,128)(2,1)} %param.10) | copy-start | bytes 98308
  127.5 12.7 %all-to-all-start.2 = ((bf16[8,256,64]{1,2,0:T(8,128)(2,1)}), bf16[8,256,64]{1,2,0:T(8,128)(2,1)S(1)}, u32[]{:S(2)}, u32[]{:S(2)}) async-start(bf16[8,256,64]{1,2,0:T(8,128)(2,1)} %copy.17), calls=%async_computation.3 | async-start | bytes 524288 | tf_op jit(solution)/shard_map/all_to_all | solution.py:52
  131.1 28.7 %reduce-scatter.8.cloned.1.call-start = ((), (), s32[]{:S(2)}) async-start(), calls=%async_computation.8 | async-start | bytes 40960 | tf_op jit(solution)/shard_map/reduce_scatter | solution.py:96
  131.2 14.4 %copy-start.1 = (bf16[768,1024]{1,0:T(8,128)(2,1)S(1)}, bf16[768,1024]{1,0:T(8,128)(2,1)}, u32[]{:S(2)}) copy-start(bf16[768,1024]{1,0:T(8,128)(2,1)} %param.6) | copy-start | bytes 4718596
  141.0 43.0 %reduce-scatter.6.cloned.1.call-start = ((), (), s32[]{:S(2)}) async-start(), calls=%async_computation.7 | async-start | bytes 655360 | tf_op jit(solution)/shard_map/reduce_scatter | solution.py:93
  145.5 105.0 %reduce-scatter.4.cloned.1.call-start = ((), (), s32[]{:S(2)}) async-start(), calls=%async_computation.6 | async-start | bytes 884736 | tf_op jit(solution)/shard_map/reduce_scatter | solution.py:76
  150.5 35.1 %all-to-all-start.1 = ((bf16[8,96,512]{2,1,0:T(8,128)(2,1)}), bf16[8,96,512]{2,1,0:T(8,128)(2,1)S(1)}, u32[]{:S(2)}, u32[]{:S(2)}) async-start(bf16[8,96,512]{2,1,0:T(8,128)(2,1)} %reshape.98), calls=%async_computation.2 | async-start | bytes 1572864 | tf_op jit(solution)/shard_map/all_to_all | solution.py:89
Sparse Core Ops, SparseCore 0:
  141.2 18.5 reduce-scatter.7
  162.3 21.6 reduce-scatter.5
  187.3 63.1 reduce-scatter.3
where the time goes:
time: 259 us
  waiting for transfers between devices  191 us (74%)
  local copies, waits for them, and re-layouts  18.8 us (7%)
  starting transfers between devices  14.8 us (6%)
  matrix products  14.4 us (6%)
  between operations  13.9 us (5%)
  other arithmetic  6.27 us (2%)
    all_to_all x1, waiting for transfers between devices, shards(): lax.all_to_all(send_tokens, 'tensor', split_axis=0, concat_axis=2, tiled=...  91.2 us
    reduce_scatter x1, waiting for transfers between devices, shards(): lax.psum_scatter(jnp.dot(tokens, frozen_value_weight, preferred_element_t...  64.8 us
    reduce_scatter x1, waiting for transfers between devices, shards(): lax.psum_scatter(local_down[None].astype(jnp.bfloat16), 'dp', scatter_dim...  22.9 us
    reshape x2, local copies, waits for them, and re-layouts, shards(): send_tokens = send_tokens.reshape(tensor_size, CAP * BLK, feature_width)  11.3 us
    all_to_all x1, starting transfers between devices, shards(): lax.all_to_all(send_tokens, 'tensor', split_axis=0, concat_axis=2, tiled=...  7.41 us
    all_to_all x1, waiting for transfers between devices, shards(): lax.all_to_all(send_cot, 'tensor', split_axis=0, concat_axis=2, tiled=True)  5.91 us
    reduce_scatter x1, waiting for transfers between devices, shards(): lax.psum_scatter(member_up_weight[None].astype(jnp.bfloat16), 'dp', scatt...  5.65 us
  transfers between devices with their start and end apart: 6, of which 5 were waited for; matrix products, arithmetic and copies ran while one was open for 7% of the time, Pallas kernels for 0%

commit v1 on v0

--- a/solution.py
+++ b/solution.py
@@ -48,7 +48,12 @@
     )
     send_cot = send_cot.reshape(tensor_size, CAP * BLK, cot_width)
     got_tokens, got_cot = (
-        lax.all_to_all(send_tokens, "tensor", split_axis=0, concat_axis=2, tiled=True),
+        jnp.concatenate(
+            lax.all_to_all(
+                jnp.stack(jnp.split(send_tokens, lax.axis_size("tensor"), axis=0)), "tensor", 0, 0
+            ),
+            axis=2,
+        ),
         lax.all_to_all(send_cot, "tensor", split_axis=0, concat_axis=2, tiled=True),
     )
     slot_tokens = got_tokens[0]

time: 259 us -> 289 us (1.12)
  local copies, waits for them, and re-layouts: 18.8 us -> 50.1 us
    another operation x0 -> x17, local copies, waits for them, and re-layouts: none -> 31.7 us  [shards(): jnp.stack(jnp.split(send_tokens, lax.axis_size('tensor'), axis=0))]
    reshape x2 -> x0, local copies, waits for them, and re-layouts: 11.3 us -> none  [shards(): send_tokens = send_tokens.reshape(tensor_size, CAP * BLK, feature_width)]
    unnamed x11 -> x32, local copies, waits for them, and re-layouts: 0.19 us -> 7.14 us
    split x0 -> x1, local copies, waits for them, and re-layouts: none -> 3.9 us  [shards(): jnp.split(send_tokens, lax.axis_size('tensor'), axis=0)]
  transfers between devices with their start and end apart: 6 -> 6, of which waited for: 5 -> 5; matrix products, arithmetic and copies ran while one was open for 7% -> 6% of each run, Pallas kernels for 0% -> 0%
where the time goes in v1:
time: 289 us; the launch traced here: 288 us
  waiting for transfers between devices  190 us (66%)
  local copies, waits for them, and re-layouts  50.1 us (17%)
  starting transfers between devices  14.9 us (5%)
  between operations  13.9 us (5%)
  matrix products  12.4 us (4%)
  other arithmetic  6.27 us (2%)
    all_to_all x1, waiting for transfers between devices, shards(): lax.all_to_all(jnp.stack(jnp.split(send_tokens, lax.axis_size('tensor'),...  91.2 us
    reduce_scatter x1, waiting for transfers between devices, shards(): lax.psum_scatter(jnp.dot(tokens, frozen_value_weight, preferred_element_t...  64.9 us
    another operation x17, local copies, waits for them, and re-layouts, shards(): jnp.stack(jnp.split(send_tokens, lax.axis_size('tensor'), axis=0))  31.7 us
    reduce_scatter x1, waiting for transfers between devices, shards(): lax.psum_scatter(local_down[None].astype(jnp.bfloat16), 'dp', scatter_dim...  22.9 us
    all_to_all x1, starting transfers between devices, shards(): lax.all_to_all(jnp.stack(jnp.split(send_tokens, lax.axis_size('tensor'),...  7.41 us
    unnamed x32, local copies, waits for them, and re-layouts  7.14 us
  transfers between devices with their start and end apart: 6, of which 5 were waited for; matrix products, arithmetic and copies ran while one was open for 6% of the time, Pallas kernels for 0%

profile of v1, /device:TPU:0, one launch (start us, length us, event | category | flops | bytes accessed | tf_op | source)
XLA Modules:
  0.0 288.0 jit_solution(7152542226470455341)
XLA Ops:
  8.9 3.4 %reshape.111 = bf16[6,131072]{1,0:T(8,128)(2,1)S(1)} reshape(bf16[768,1024]{1,0:T(8,128)(2,1)} %param.6) | data formatting | bytes 3145728 | tf_op jit(solution)/shard_map/reshape | solution.py:40
  13.5 3.9 %fusion.15 = (bf16[2,131072]{1,0:T(2,128)(2,1)S(1)}, bf16[2,131072]{1,0:T(2,128)(2,1)S(1)}, bf16[2,131072]{1,0:T(2,128)(2,1)S(1)}, bf16[2,131072]{1,0:T(2,128)(2...) fusion(bf16[16,131072]{1,0:T(8,128)(2,1)S(1)} %convolution_conv, ...), kind=kLoop, calls=%fused_computation.38 | loop fusion | bytes 8388608 | tf_op jit(solution)/shard_map/split | solution.py:53
  17.4 2.3 stack.27
  19.7 2.0 copy.30
  23.6 2.3 stack.28
  27.9 2.3 stack.29
  30.2 2.0 copy.32
  32.3 2.3 stack.30
  34.6 2.1 copy.33
  38.0 2.1 copy.34
  41.3 2.1 copy.35
  44.7 2.1 copy.36
  48.1 2.1 copy.37
  56.1 7.4 %all-to-all-start = ((bf16[8,1,256,1024]{2,3,1,0:T(8,128)(2,1)}), bf16[8,1,256,1024]{2,3,1,0:T(8,128)(2,1)}, u32[]{:S(2)}, u32[]{:S(2)}) async-start(bf16[8,1,256,1024]{2,3,1,0:T(8,128)(2,1)} %constant_dynamic-update-slice_fusion), calls=%async_computation.1 | async-start | bytes 8388608 | tf_op jit(solution)/shard_map/all_to_all | solution.py:52
  65.5 91.2 %all-to-all-done = bf16[8,1,256,1024]{2,3,1,0:T(8,128)(2,1)} async-done(((bf16[8,1,256,1024]{2,3,1,0:T(8,128)(2,1)}), bf16[8,1,256,1024]{2,3,1,0:T(8,128)(2,1)}, u32[]{:S(2)}, u32[]{:S(2)}) %all-to-all-start) | async-done | bytes 4194336 | tf_op jit(solution)/shard_map/all_to_all | solution.py:52
  156.8 3.6 %all-to-all-start.2 = ((bf16[8,256,64]{1,2,0:T(8,128)(2,1)}), bf16[8,256,64]{1,2,0:T(8,128)(2,1)S(1)}, u32[]{:S(2)}, u32[]{:S(2)}) async-start(bf16[8,256,64]{1,2,0:T(8,128)(2,1)} %copy.40), calls=%async_computation.3 | async-start | bytes 524288 | tf_op jit(solution)/shard_map/all_to_all | solution.py:57
  160.7 3.1 %convolution_convert_fusion.5 = bf16[256,32]{0,1:T(8,128)(2,1)S(1)} fusion(bf16[256,8192]{0,1:T(8,128)(2,1)} %bitcast.4, bf16[1,32,8192]{2,1,0:T(8,128)(2,1)S(1)} %copy-done.9), kind=kOutput, calls=%fused_computation.14 | convolution fusion | flops 134225920 | bytes 4734976 | tf_op jit(solution)/shard_map/dot_general | solution.py:63
  163.8 5.7 %all-to-all-done.2 = bf16[8,256,64]{1,2,0:T(8,128)(2,1)S(1)} async-done(((bf16[8,256,64]{1,2,0:T(8,128)(2,1)}), bf16[8,256,64]{1,2,0:T(8,128)(2,1)S(1)}, u32[]{:S(2)}, u32[]{:S(2)}) %all-to-all-start.2) | async-done | bytes 262176 | tf_op jit(solution)/shard_map/all_to_all | solution.py:57
  170.4 4.4 %fusion = bf16[1,32,8192]{2,1,0:T(8,128)(2,1)} fusion(bf16[256,8192]{0,1:T(8,128)(2,1)} %bitcast.4, bf16[256,512]{0,1:T(8,128)(2,1)S(1)} %bitcast.41, bf16[1,32,512]{2,1,0:T(8,128)(2,1)S(1)} %copy-done.10), kind=kOutput, calls=%fused_computation.3 | convolution fusion | flops 142884864 | bytes 5013504 | tf_op jit(solution)/shard_map/dot_general | solution.py:75
  177.8 2.1 reshape.114
  179.9 3.6 %all-to-all-start.1 = ((bf16[8,96,512]{2,1,0:T(8,128)(2,1)}), bf16[8,96,512]{2,1,0:T(8,128)(2,1)S(1)}, u32[]{:S(2)}, u32[]{:S(2)}) async-start(bf16[8,96,512]{2,1,0:T(8,128)(2,1)} %reshape.114), calls=%async_computation.2 | async-start | bytes 1572864 | tf_op jit(solution)/shard_map/all_to_all | solution.py:94
  183.5 5.6 %reduce-scatter.8.cloned.1.call-done = bf16[1,8,512]{2,1,0:T(8,128)(2,1)} async-done(((bf16[1,32,512]{2,1,0:T(8,128)(2,1)}), bf16[1,8,512]{2,1,0:T(8,128)(2,1)}) %reduce-scatter.8.cloned.1.call-update) | async-done | bytes 8208 | tf_op jit(solution)/shard_map/reduce_scatter | solution.py:101
  190.4 22.9 %reduce-scatter.6.cloned.1.call-done = bf16[1,32,2048]{2,1,0:T(8,128)(2,1)} async-done(((bf16[1,32,8192]{2,1,0:T(8,128)(2,1)}), bf16[1,32,2048]{2,1,0:T(8,128)(2,1)}) %reduce-scatter.6.cloned.1.call-update) | async-done | bytes 131088 | tf_op jit(solution)/shard_map/reduce_scatter | solution.py:98
  215.0 64.9 %reduce-scatter.4.cloned.1.call-done = bf16[96,512]{1,0:T(8,128)(2,1)} async-done(((bf16[768,512]{1,0:T(8,128)(2,1)}), bf16[96,512]{1,0:T(8,128)(2,1)}) %reduce-scatter.4.cloned.1.call-update) | async-done | bytes 98320 | tf_op jit(solution)/shard_map/reduce_scatter | solution.py:81
  (64 shorter events, 28.4 us)
Async XLA Ops:
  7.2 167.7 %copy-start = (bf16[1024,512]{1,0:T(8,128)(2,1)S(1)}, bf16[1024,512]{1,0:T(8,128)(2,1)}, u32[]{:S(2)}) copy-start(bf16[1024,512]{1,0:T(8,128)(2,1)} %param.8) | copy-start | bytes 3145732
  38.0 12.2 %copy-start.1 = (bf16[1,1,256,1024]{2,3,1,0:T(8,128)(2,1)S(1)}, bf16[1,1,256,1024]{2,3,1,0:T(8,128)(2,1)}, u32[]{:S(2)}) copy-start(bf16[1,1,256,1024]{2,3,1,0:T(8,128)(2,1)} %copy.31) | copy-start | bytes 1572868
  41.3 9.7 %copy-start.2 = (bf16[1,1,256,1024]{2,3,1,0:T(8,128)(2,1)S(1)}, bf16[1,1,256,1024]{2,3,1,0:T(8,128)(2,1)}, u32[]{:S(2)}) copy-start(bf16[1,1,256,1024]{2,3,1,0:T(8,128)(2,1)} %copy.32) | copy-start | bytes 1572868
  44.7 7.2 %copy-start.3 = (bf16[1,1,256,1024]{2,3,1,0:T(8,128)(2,1)S(1)}, bf16[1,1,256,1024]{2,3,1,0:T(8,128)(2,1)}, u32[]{:S(2)}) copy-start(bf16[1,1,256,1024]{2,3,1,0:T(8,128)(2,1)} %copy.33) | copy-start | bytes 1572868
  48.1 4.6 %copy-start.4 = (bf16[1,1,256,1024]{2,3,1,0:T(8,128)(2,1)S(1)}, bf16[1,1,256,1024]{2,3,1,0:T(8,128)(2,1)}, u32[]{:S(2)}) copy-start(bf16[1,1,256,1024]{2,3,1,0:T(8,128)(2,1)} %copy.34) | copy-start | bytes 1572868
  50.2 3.4 %copy-start.5 = (bf16[1,1,256,1024]{2,3,1,0:T(8,128)(2,1)S(1)}, bf16[1,1,256,1024]{2,3,1,0:T(8,128)(2,1)}, u32[]{:S(2)}) copy-start(bf16[1,1,256,1024]{2,3,1,0:T(8,128)(2,1)} %copy.35) | copy-start | bytes 1572868
  50.2 4.2 %copy-start.6 = (bf16[1,1,256,1024]{2,3,1,0:T(8,128)(2,1)S(1)}, bf16[1,1,256,1024]{2,3,1,0:T(8,128)(2,1)}, u32[]{:S(2)}) copy-start(bf16[1,1,256,1024]{2,3,1,0:T(8,128)(2,1)} %copy.36) | copy-start | bytes 1572868
  50.2 5.1 %copy-start.7 = (bf16[1,1,256,1024]{2,3,1,0:T(8,128)(2,1)S(1)}, bf16[1,1,256,1024]{2,3,1,0:T(8,128)(2,1)}, u32[]{:S(2)}) copy-start(bf16[1,1,256,1024]{2,3,1,0:T(8,128)(2,1)} %copy.37) | copy-start | bytes 1572868
  56.1 7.4 %copy-start.11 = (bf16[768,64]{0,1:T(8,128)(2,1)S(1)}, bf16[768,64]{0,1:T(8,128)(2,1)}, u32[]{:S(2)}) copy-start(bf16[768,64]{0,1:T(8,128)(2,1)} %param.7) | copy-start | bytes 294916
  56.1 104.6 %copy-start.9 = (bf16[1,32,8192]{2,1,0:T(8,128)(2,1)S(1)}, bf16[1,32,8192]{2,1,0:T(8,128)(2,1)}, u32[]{:S(2)}) copy-start(bf16[1,32,8192]{2,1,0:T(8,128)(2,1)} %param.9) | copy-start | bytes 1572868
  56.1 100.7 %all-to-all-start = ((bf16[8,1,256,1024]{2,3,1,0:T(8,128)(2,1)}), bf16[8,1,256,1024]{2,3,1,0:T(8,128)(2,1)}, u32[]{:S(2)}, u32[]{:S(2)}) async-start(bf16[8,1,256,1024]{2,3,1,0:T(8,128)(2,1)} %constant_dynamic-update-slice_fusion), calls=%async_computation.1 | async-start | bytes 8388608 | tf_op jit(solution)/shard_map/all_to_all | solution.py:52
  63.5 106.9 %copy-start.10 = (bf16[1,32,512]{2,1,0:T(8,128)(2,1)S(1)}, bf16[1,32,512]{2,1,0:T(8,128)(2,1)}, u32[]{:S(2)}) copy-start(bf16[1,32,512]{2,1,0:T(8,128)(2,1)} %param.10) | copy-start | bytes 98308
  156.8 12.7 %all-to-all-start.2 = ((bf16[8,256,64]{1,2,0:T(8,128)(2,1)}), bf16[8,256,64]{1,2,0:T(8,128)(2,1)S(1)}, u32[]{:S(2)}, u32[]{:S(2)}) async-start(bf16[8,256,64]{1,2,0:T(8,128)(2,1)} %copy.40), calls=%async_computation.3 | async-start | bytes 524288 | tf_op jit(solution)/shard_map/all_to_all | solution.py:57
  160.4 28.7 %reduce-scatter.8.cloned.1.call-start = ((), (), s32[]{:S(2)}) async-start(), calls=%async_computation.8 | async-start | bytes 40960 | tf_op jit(solution)/shard_map/reduce_scatter | solution.py:101
  160.7 14.2 %copy-start.8 = (bf16[768,1024]{1,0:T(8,128)(2,1)S(1)}, bf16[768,1024]{1,0:T(8,128)(2,1)}, u32[]{:S(2)}) copy-start(bf16[768,1024]{1,0:T(8,128)(2,1)} %param.6) | copy-start | bytes 4718596
  170.3 43.0 %reduce-scatter.6.cloned.1.call-start = ((), (), s32[]{:S(2)}) async-start(), calls=%async_computation.7 | async-start | bytes 655360 | tf_op jit(solution)/shard_map/reduce_scatter | solution.py:98
  174.8 105.1 %reduce-scatter.4.cloned.1.call-start = ((), (), s32[]{:S(2)}) async-start(), calls=%async_computation.6 | async-start | bytes 884736 | tf_op jit(solution)/shard_map/reduce_scatter | solution.py:81
  179.9 35.0 %all-to-all-start.1 = ((bf16[8,96,512]{2,1,0:T(8,128)(2,1)}), bf16[8,96,512]{2,1,0:T(8,128)(2,1)S(1)}, u32[]{:S(2)}, u32[]{:S(2)}) async-start(bf16[8,96,512]{2,1,0:T(8,128)(2,1)} %reshape.114), calls=%async_computation.2 | async-start | bytes 1572864 | tf_op jit(solution)/shard_map/all_to_all | solution.py:94
Sparse Core Ops, SparseCore 0:
  170.5 18.5 reduce-scatter.7
  191.6 21.6 reduce-scatter.5
  216.6 63.2 reduce-scatter.3
